TPU v7x, 512 devices: a whole 4x4x16 slice. The times are simulated.
512 devices in a mesh: sec: 2 (over z_hi), gx: 16 (over z_lo, core), gy: 16 (over x, y).
Axes of the slice: x: 4, y: 4, z: 16 (z_hi: 2, z_lo: 8; z = z_hi * 8 + z_lo), core: 2. Of those that a mesh axis runs over, the one named last changes fastest.
Arguments:
- terminal: float32 [4, 16, 256, 4096], P('sec', None, 'gx', 'gy'), may hold values from -6 to 6
- forward_temp: bfloat16 [2, 4, 16, 256, 4096], P(None, 'sec', None, 'gx', 'gy'), may hold values from -6 to 6
- conductivity: float32 [16, 256, 4096], P(None, 'gx', 'gy'), may hold values from 0.02 to 0.15
- velocity: float32 [2, 16, 256, 4096], P(None, None, 'gx', 'gy'), may hold values from -0.3 to 0.3
- fixed_mask: int32 [16, 256, 4096], P(None, 'gx', 'gy'), may hold values 0 or 1
- wells: int32 [4, 8, 3], P('sec'), may hold values from 0 to 4095, as said below
- misfit: float32 [2, 4, 8], P(None, 'sec'), may hold values from -12 to 12
- head_gradient: bfloat16 [2, 16, 256, 4096], P('sec', None, 'gx', 'gy'), may hold values from -6 to 6
- blocks: bfloat16 [32, 7, 128, 128], P('gy'), may hold values from -0.1875 to 0.1875
- block_cols: int32 [32, 7], P('gy'), may hold values from 0 to 31, as said below
Outputs:
- head_adjoint: float32 [2, 16, 256, 4096], P('sec', None, 'gx', 'gy')
- sensitivity: float32 [16, 256, 4096], P(None, 'gx', 'gy')
Inputs may be any that keep to these rules, and one draw needn't show every extreme that they name: `wells`: each row is one cell (z, x, y) with z < 16, x < 256, y < 4096; the first test observes the cells (0, 0, 0) and (15, 255, 4095). `block_cols`: row r lists 7 different block columns, the first of which is r.
All inputs are finite; a program needn't handle non-finite values. No bound on the sum of `fixed_mask` on one device may be relied on, other than what follows from the above.
Results may differ from a plain program's by a relative error of at most 0.0029.
Values may be sent and summed in bfloat16 or wider, within the bound.
No kernel may reach another device: no remote copies, remote signals or barrier semaphores. Data moves between devices by JAX's collectives and lax.ppermute only.
A program may use at most 64 MiB of HBM per device.

v0:
```python
import jax
import jax.numpy as jnp
from jax import lax
from jax.sharding import PartitionSpec as P


def extended(cells, sides, width):
    for axis, dim in sides:
        count = lax.axis_size(axis)
        ends = count - 1
        head = lax.slice_in_dim(cells, 0, width, axis=dim)
        tail = lax.slice_in_dim(cells, cells.shape[dim] - width, cells.shape[dim], axis=dim)
        cells = jnp.concatenate(
            [
                lax.ppermute(tail, axis, [(i, (i + 1) % count) for i in range(ends)]),
                cells,
                lax.ppermute(head, axis, [((i + 1) % count, i) for i in range(ends)]),
            ],
            axis=dim,
        )
    return cells


def shifted(padded):
    lead = [(0, 0)] * (padded.ndim - 3)
    deeper = jnp.pad(padded, lead + [(1, 1), (0, 0), (0, 0)])
    centre = deeper[..., 1:-1, 1:-1, 1:-1]
    beside_all = [
        deeper[..., 2:, 1:-1, 1:-1],
        deeper[..., :-2, 1:-1, 1:-1],
        deeper[..., 1:-1, 2:, 1:-1],
        deeper[..., 1:-1, :-2, 1:-1],
        deeper[..., 1:-1, 1:-1, 2:],
        deeper[..., 1:-1, 1:-1, :-2],
    ]
    return (centre, beside_all)


def face_weights(kappa_pad):
    centre, beside_all = shifted(kappa_pad)
    return [
        2.0 * centre * other / jnp.where(centre + other > 0.0, centre + other, 1.0)
        for other in beside_all
    ]


def advance(adjoint_pad, weights, keep, speed_x, speed_y, source):
    centre, beside_all = shifted(adjoint_pad)
    diffusion = weights[0] * (beside_all[0] - centre)
    for face in range(1, 6):
        diffusion = diffusion + weights[face] * (beside_all[face] - centre)
    slope_x = 0.5 * (beside_all[2] - beside_all[3])
    slope_y = 0.5 * (beside_all[4] - beside_all[5])
    updated = keep * (centre + diffusion + speed_x * slope_x + speed_y * slope_y + source)
    return (updated, diffusion, slope_x, slope_y)


def well_sources(wells, misfit_level, layers, rows_x, cols_y, margin):
    start_x = lax.axis_index("gx") * rows_x - margin
    start_y = lax.axis_index("gy") * cols_y - margin
    coord_z = jnp.arange(layers, dtype=jnp.int32)[:, None, None]
    coord_x = (start_x + jnp.arange(rows_x + 2 * margin, dtype=jnp.int32))[None, :, None]
    coord_y = (start_y + jnp.arange(cols_y + 2 * margin, dtype=jnp.int32))[None, None, :]
    well_z = wells[:, :, 0][:, :, None, None, None]
    well_x = wells[:, :, 1][:, :, None, None, None]
    well_y = wells[:, :, 2][:, :, None, None, None]
    matches = (coord_z == well_z) & (coord_x == well_x) & (coord_y == well_y)
    return jnp.sum(jnp.where(matches, misfit_level[:, :, None, None, None], 0.0), axis=1)


def shards(
    terminal,
    forward_temp,
    conductivity,
    velocity,
    fixed_mask,
    wells,
    misfit,
    head_gradient,
    blocks,
    block_cols,
):
    layers, rows_x, cols_y = conductivity.shape
    steps = forward_temp.shape[0]
    keep = 1.0 - fixed_mask.astype(jnp.float32)
    heat_sens = jnp.zeros((layers, rows_x, cols_y), jnp.float32)
    flow_x = jnp.zeros((layers, rows_x, cols_y), jnp.float32)
    flow_y = jnp.zeros((layers, rows_x, cols_y), jnp.float32)
    kappa_pad = extended(conductivity, (("gx", 1), ("gy", 2)), 1)
    weights = face_weights(kappa_pad)
    adjoint = terminal
    for level in reversed(range(steps)):
        padded = extended(adjoint, (("gx", 2), ("gy", 3)), 1)
        source = well_sources(wells, misfit[level], layers, rows_x, cols_y, 0)
        adjoint, diffusion, slope_x, slope_y = advance(
            padded, weights, keep, velocity[0], velocity[1], source
        )
        temper = forward_temp[level].astype(jnp.float32)
        heat_sens = heat_sens + jnp.sum(temper * diffusion, axis=0)
        flow_x = flow_x + jnp.sum(temper * slope_x, axis=0)
        flow_y = flow_y + jnp.sum(temper * slope_y, axis=0)
    summed = lax.psum_scatter(jnp.stack([flow_x, flow_y]), "sec", scatter_dimension=0, tiled=True)
    rounded = summed[0].astype(jnp.bfloat16)
    row_blocks, per_row, block_size, _ = blocks.shape
    piece = lax.all_gather(rounded, "gy", axis=2, tiled=True)
    count = piece.shape[2] // block_size
    split_rows = piece.reshape(layers, rows_x, count, block_size)
    block_ids = jnp.arange(count, dtype=jnp.int32)
    chosen = (block_cols[:, :, None] == block_ids[None, None, :]).astype(jnp.bfloat16)
    portion = jnp.einsum("bkq,zxqj->bkzxj", chosen, split_rows, preferred_element_type=jnp.float32)
    picked = portion.astype(jnp.bfloat16)
    head = jnp.einsum(
        "bkzxj,bkij->zxbi", picked, blocks, preferred_element_type=jnp.float32
    ).reshape(layers, rows_x, cols_y)
    partial_sens = heat_sens + head * head_gradient[0].astype(jnp.float32)
    sensitivity = lax.psum(partial_sens, "sec")
    return (head[None], sensitivity)


def solution(mesh):
    placed = (
        P("sec", None, "gx", "gy"),
        P(None, "sec", None, "gx", "gy"),
        P(None, "gx", "gy"),
        P(None, None, "gx", "gy"),
        P(None, "gx", "gy"),
        P("sec", None, None),
        P(None, "sec", None),
        P("sec", None, "gx", "gy"),
        P("gy", None, None, None),
        P("gy", None),
    )
    return jax.shard_map(
        shards,
        mesh=mesh,
        in_specs=placed,
        out_specs=(P("sec", None, "gx", "gy"), P(None, "gx", "gy")),
        check_vma=False,
    )
```

profile of v0, /device:TPU:1, one launch (start us, length us, event | category | flops | bytes accessed | tf_op | source)
XLA Modules:
  0.0 278.9 jit_solution(739867863807899032)
XLA Ops:
  7.2 0.0 reduce-scatter.2.cloned.1.call-start
  7.3 1.1 fusion.57
  8.3 4.9 %collective-permute-start.2 = (f32[16,1,256]{2,1,0:T(1,128)S(1)}, f32[16,1,256]{2,1,0:T(1,128)S(1)}, u32[]{:S(2)}, u32[]{:S(2)}) collective-permute-start(f32[16,1,256]{2,1,0:T(1,128)S(1)} %get-tuple-element.29), channel_id=1, source_target_pairs={{0,16},{16,32},{32,48},{48,64},{64,80},{80,96},{96,112},{112,128},... | collective-permute-start | bytes 49160 | tf_op jit(solution)/shard_map/ppermute | solution.py:15
  13.3 5.1 %collective-permute-start.3 = (f32[16,1,256]{2,1,0:T(1,128)S(1)}, f32[16,1,256]{2,1,0:T(1,128)S(1)}, u32[]{:S(2)}, u32[]{:S(2)}) collective-permute-start(f32[16,1,256]{2,1,0:T(1,128)S(1)} %get-tuple-element.30), channel_id=1, source_target_pairs={{16,0},{32,16},{48,32},{64,48},{80,64},{96,80},{112,96},{128,112},... | collective-permute-start | bytes 49160 | tf_op jit(solution)/shard_map/ppermute | solution.py:17
  18.4 1.1 fusion.55
  19.5 1.9 collective-permute-start
  21.4 3.6 %collective-permute-start.1 = (f32[2,16,1,256]{3,2,1,0:T(1,128)S(1)}, f32[2,16,1,256]{3,2,1,0:T(1,128)S(1)}, u32[]{:S(2)}, u32[]{:S(2)}) collective-permute-start(f32[2,16,1,256]{3,2,1,0:T(1,128)S(1)} %get-tuple-element.20), channel_id=1, source_target_pairs={{0,16},{16,32},{32,48},{48,64},{64,80},{80,96},{96,112},{112,128},... | collective-permute-start | bytes 98312 | tf_op jit(solution)/shard_map/ppermute | solution.py:15
  25.1 0.7 slice_bitcast_fusion.3
  25.8 0.1 iota_compare_fusion.4
  25.9 1.1 multiply_bitcast_fusion.1
  27.0 0.1 broadcast_compare_fusion.1
  27.1 0.1 broadcast_and_fusion
  27.2 0.1 broadcast_compare_fusion
  27.3 0.1 pad_maximum_fusion.19
  27.4 0.1 fusion.56
  27.5 1.4 collective-permute-start.4
  28.9 1.3 collective-permute-start.5
  30.2 0.8 select_reduce_fusion
  31.1 1.5 collective-permute-done.4
  32.6 4.1 %collective-permute-done.5 = f32[16,18,1]{2,1,0:T(8,128)S(1)} collective-permute-done((f32[16,18,1]{2,1,0:T(8,128)S(1)}, f32[16,18,1]{2,1,0:T(8,128)S(1)}, u32[]{:S(2)}, u32[]{:S(2)}) %collective-permute-start.5) | collective-permute-done | bytes 1184 | tf_op jit(solution)/shard_map/ppermute | solution.py:17
  36.7 0.4 select_maximum_fusion.8
  37.1 0.1 pad_maximum_fusion
  37.2 0.2 fusion.53
  37.4 2.2 collective-permute-start.6
  39.6 1.3 collective-permute-start.7
  40.9 0.6 fusion.41
  41.5 6.3 %collective-permute-done.6 = f32[2,16,18,1]{3,2,1,0:T(8,128)S(1)} collective-permute-done((f32[2,16,18,1]{3,2,1,0:T(8,128)S(1)}, f32[2,16,18,1]{3,2,1,0:T(8,128)S(1)}, u32[]{:S(2)}, u32[]{:S(2)}) %collective-permute-start.6) | collective-permute-done | bytes 2336 | tf_op jit(solution)/shard_map/ppermute | solution.py:15
  47.8 3.8 %collective-permute-done.7 = f32[2,16,18,1]{3,2,1,0:T(8,128)S(1)} collective-permute-done((f32[2,16,18,1]{3,2,1,0:T(8,128)S(1)}, f32[2,16,18,1]{3,2,1,0:T(8,128)S(1)}, u32[]{:S(2)}, u32[]{:S(2)}) %collective-permute-start.7) | collective-permute-done | bytes 2336 | tf_op jit(solution)/shard_map/ppermute | solution.py:17
  51.6 0.7 select_maximum_fusion.4
  52.3 1.1 add_multiply_fusion
  53.5 3.3 %collective-permute-start.8 = (f32[2,16,1,256]{3,2,1,0:T(1,128)S(1)}, f32[2,16,1,256]{3,2,1,0:T(1,128)S(1)}, u32[]{:S(2)}, u32[]{:S(2)}) collective-permute-start(f32[2,16,1,256]{3,2,1,0:T(1,128)S(1)} %get-tuple-element.15), channel_id=1, source_target_pairs={{16,0},{32,16},{48,32},{64,48},{80,64},{96,80},{112,96},{128,112},... | collective-permute-start | bytes 98312 | tf_op jit(solution)/shard_map/ppermute | solution.py:17
  56.8 3.8 %collective-permute-start.9 = (f32[2,16,1,256]{3,2,1,0:T(1,128)S(1)}, f32[2,16,1,256]{3,2,1,0:T(1,128)S(1)}, u32[]{:S(2)}, u32[]{:S(2)}) collective-permute-start(f32[2,16,1,256]{3,2,1,0:T(1,128)S(1)} %get-tuple-element.16), channel_id=1, source_target_pairs={{0,16},{16,32},{32,48},{48,64},{64,80},{80,96},{96,112},{112,128},... | collective-permute-start | bytes 98312 | tf_op jit(solution)/shard_map/ppermute | solution.py:15
  60.6 1.0 collective-permute-done.9
  61.6 0.1 pad_maximum_fusion.1
  61.7 0.2 fusion.52
  61.9 1.3 collective-permute-start.10
  63.2 5.1 %collective-permute-start.11 = (f32[2,16,18,1]{3,2,1,0:T(8,128)S(1)}, f32[2,16,18,1]{3,2,1,0:T(8,128)S(1)}, u32[]{:S(2)}, u32[]{:S(2)}) collective-permute-start(f32[2,16,18,1]{3,2,1,0:T(8,128)S(1)} %get-tuple-element.12), channel_id=1, source_target_pairs={{0,1},{1,2},{2,3},{3,4},{4,5},{5,6},{6,7},{7,8},{8,9},{9,10},{10,1... | collective-permute-start | bytes 6920 | tf_op jit(solution)/shard_map/ppermute | solution.py:15
  68.3 0.6 fusion.4
  68.9 5.6 %collective-permute-done.10 = f32[2,16,18,1]{3,2,1,0:T(8,128)S(1)} collective-permute-done((f32[2,16,18,1]{3,2,1,0:T(8,128)S(1)}, f32[2,16,18,1]{3,2,1,0:T(8,128)S(1)}, u32[]{:S(2)}, u32[]{:S(2)}) %collective-permute-start.10) | collective-permute-done | bytes 2336 | tf_op jit(solution)/shard_map/ppermute | solution.py:17
  74.5 1.8 collective-permute-done.11
  76.2 1.3 fusion.7
  77.5 0.1 add_bitcast_fusion
  77.6 0.8 pad_maximum_fusion.18
  78.5 0.0 reduce-scatter.2.cloned.1.call-update
  78.5 0.0 all-gather.3.cloned.1.call-start
  78.5 59.7 %reduce-scatter.2.cloned.1.call-done = f32[1,16,16,256]{3,2,1,0:T(8,128)} async-done(((f32[2,16,16,256]{3,2,1,0:T(8,128)}), f32[1,16,16,256]{3,2,1,0:T(8,128)}) %reduce-scatter.2.cloned.1.call-update) | async-done | bytes 262160 | tf_op jit(solution)/shard_map/reduce_scatter | solution.py:102
  138.3 1.6 convert_element_type.41
  139.9 0.0 all-gather.3.cloned.1.call-update
  139.9 0.0 all-reduce.5.cloned.1.call-start
  140.0 0.7 select_maximum_fusion
  140.7 0.3 copy-done.4
  141.0 1.7 fusion.9
  142.7 52.4 %all-gather.3.cloned.1.call-done = bf16[1,16,16,4096]{3,2,1,0:T(8,128)(2,1)} async-done(((bf16[1,16,16,256]{3,2,1,0:T(8,128)(2,1)}), bf16[1,16,16,4096]{3,2,1,0:T(8,128)(2,1)}) %all-gather.3.cloned.1.call-update) | async-done | bytes 2097168 | tf_op jit(solution)/shard_map/all_gather | solution.py:105
  195.1 2.1 copy.21
  197.2 0.5 convolution_convert_fusion
  197.8 0.4 fusion.1
  198.2 0.5 copy-done.5
  198.7 0.1 copy-done.6
  198.8 0.0 copy-done.8
  198.8 0.8 fusion.43
  199.6 0.2 copy.15
  199.8 0.9 broadcast_in_dim_reshape.3
  200.7 70.0 %all-reduce.5.cloned.1.call-done = f32[16,16,256]{2,1,0:T(8,128)} async-done(((f32[16,16,256]{2,1,0:T(8,128)}), f32[16,16,256]{2,1,0:T(8,128)}) %all-reduce.5.cloned.1.call-update) | async-done | bytes 262160 | tf_op jit(solution)/shard_map/psum | solution.py:116
  270.7 1.7 copy.26
  (29 shorter events, 0.2 us)
Async XLA Ops:
  7.2 190.6 %copy-start = (bf16[2,7,128,128]{3,2,1,0:T(8,128)(2,1)S(1)}, bf16[2,7,128,128]{3,2,1,0:T(8,128)(2,1)}, u32[]{:S(2)}) copy-start(bf16[2,7,128,128]{3,2,1,0:T(8,128)(2,1)} %param.18) | copy-start | bytes 1376260
  7.2 20.1 %copy-start.2 = (f32[16,16,256]{2,1,0:T(8,128)S(1)}, f32[16,16,256]{2,1,0:T(8,128)}, u32[]{:S(2)}) copy-start(f32[16,16,256]{2,1,0:T(8,128)} %param.12) | copy-start | bytes 786436
  7.2 19.8 %copy-start.7 = (s32[16,16,256]{2,1,0:T(8,128)S(1)}, s32[16,16,256]{2,1,0:T(8,128)}, u32[]{:S(2)}) copy-start(s32[16,16,256]{2,1,0:T(8,128)} %param.14) | copy-start | bytes 786436
  7.2 20.1 %copy-start.10 = (f32[2,2,8]{2,1,0:T(2,128)S(1)}, f32[2,2,8]{2,1,0:T(2,128)}, u32[]{:S(2)}) copy-start(f32[2,2,8]{2,1,0:T(2,128)} %param.16) | copy-start | bytes 388
  7.2 131.1 %reduce-scatter.2.cloned.1.call-start = ((), (), s32[]{:S(2)}) async-start(), calls=%async_computation.1 | async-start | bytes 786432 | tf_op jit(solution)/shard_map/reduce_scatter | solution.py:102
  8.3 18.9 %collective-permute-start.2 = (f32[16,1,256]{2,1,0:T(1,128)S(1)}, f32[16,1,256]{2,1,0:T(1,128)S(1)}, u32[]{:S(2)}, u32[]{:S(2)}) collective-permute-start(f32[16,1,256]{2,1,0:T(1,128)S(1)} %get-tuple-element.29), channel_id=1, source_target_pairs={{0,16},{16,32},{32,48},{48,64},{64,80},{80,96},{96,112},{112,128},... | collective-permute-start | bytes 49160 | tf_op jit(solution)/shard_map/ppermute | solution.py:15
  13.3 14.0 %collective-permute-start.3 = (f32[16,1,256]{2,1,0:T(1,128)S(1)}, f32[16,1,256]{2,1,0:T(1,128)S(1)}, u32[]{:S(2)}, u32[]{:S(2)}) collective-permute-start(f32[16,1,256]{2,1,0:T(1,128)S(1)} %get-tuple-element.30), channel_id=1, source_target_pairs={{16,0},{32,16},{48,32},{64,48},{80,64},{96,80},{112,96},{128,112},... | collective-permute-start | bytes 49160 | tf_op jit(solution)/shard_map/ppermute | solution.py:17
  19.5 17.6 %collective-permute-start = (f32[2,16,1,256]{3,2,1,0:T(1,128)S(1)}, f32[2,16,1,256]{3,2,1,0:T(1,128)S(1)}, u32[]{:S(2)}, u32[]{:S(2)}) collective-permute-start(f32[2,16,1,256]{3,2,1,0:T(1,128)S(1)} %get-tuple-element.19), channel_id=1, source_target_pairs={{16,0},{32,16},{48,32},{64,48},{80,64},{96,80},{112,96},{128,112},... | collective-permute-start | bytes 98312 | tf_op jit(solution)/shard_map/ppermute | solution.py:17
  21.4 15.7 %collective-permute-start.1 = (f32[2,16,1,256]{3,2,1,0:T(1,128)S(1)}, f32[2,16,1,256]{3,2,1,0:T(1,128)S(1)}, u32[]{:S(2)}, u32[]{:S(2)}) collective-permute-start(f32[2,16,1,256]{3,2,1,0:T(1,128)S(1)} %get-tuple-element.20), channel_id=1, source_target_pairs={{0,16},{16,32},{32,48},{48,64},{64,80},{80,96},{96,112},{112,128},... | collective-permute-start | bytes 98312 | tf_op jit(solution)/shard_map/ppermute | solution.py:15
  27.4 9.7 %copy-start.1 = (f32[2,16,16,256]{3,2,1,0:T(8,128)S(1)}, f32[2,16,16,256]{3,2,1,0:T(8,128)}, u32[]{:S(2)}) copy-start(f32[2,16,16,256]{3,2,1,0:T(8,128)} %param.10) | copy-start | bytes 1572868
  27.5 5.1 %collective-permute-start.4 = (f32[16,18,1]{2,1,0:T(8,128)S(1)}, f32[16,18,1]{2,1,0:T(8,128)S(1)}, u32[]{:S(2)}, u32[]{:S(2)}) collective-permute-start(f32[16,18,1]{2,1,0:T(8,128)S(1)} %get-tuple-element.22), channel_id=1, source_target_pairs={{0,1},{1,2},{2,3},{3,4},{4,5},{5,6},{6,7},{7,8},{8,9},{9,10},{10,1... | collective-permute-start | bytes 3464 | tf_op jit(solution)/shard_map/ppermute | solution.py:15
  28.9 7.8 %collective-permute-start.5 = (f32[16,18,1]{2,1,0:T(8,128)S(1)}, f32[16,18,1]{2,1,0:T(8,128)S(1)}, u32[]{:S(2)}, u32[]{:S(2)}) collective-permute-start(f32[16,18,1]{2,1,0:T(8,128)S(1)} %get-tuple-element.21), channel_id=1, source_target_pairs={{1,0},{2,1},{3,2},{4,3},{5,4},{6,5},{7,6},{8,7},{9,8},{10,9},{11,1... | collective-permute-start | bytes 3464 | tf_op jit(solution)/shard_map/ppermute | solution.py:17
  37.4 10.4 %collective-permute-start.6 = (f32[2,16,18,1]{3,2,1,0:T(8,128)S(1)}, f32[2,16,18,1]{3,2,1,0:T(8,128)S(1)}, u32[]{:S(2)}, u32[]{:S(2)}) collective-permute-start(f32[2,16,18,1]{3,2,1,0:T(8,128)S(1)} %get-tuple-element.14), channel_id=1, source_target_pairs={{0,1},{1,2},{2,3},{3,4},{4,5},{5,6},{6,7},{7,8},{8,9},{9,10},{10,1... | collective-permute-start | bytes 6920 | tf_op jit(solution)/shard_map/ppermute | solution.py:15
  39.6 12.0 %collective-permute-start.7 = (f32[2,16,18,1]{3,2,1,0:T(8,128)S(1)}, f32[2,16,18,1]{3,2,1,0:T(8,128)S(1)}, u32[]{:S(2)}, u32[]{:S(2)}) collective-permute-start(f32[2,16,18,1]{3,2,1,0:T(8,128)S(1)} %get-tuple-element.13), channel_id=1, source_target_pairs={{1,0},{2,1},{3,2},{4,3},{5,4},{6,5},{7,6},{8,7},{9,8},{10,9},{11,1... | collective-permute-start | bytes 6920 | tf_op jit(solution)/shard_map/ppermute | solution.py:17
  53.5 7.1 %collective-permute-start.8 = (f32[2,16,1,256]{3,2,1,0:T(1,128)S(1)}, f32[2,16,1,256]{3,2,1,0:T(1,128)S(1)}, u32[]{:S(2)}, u32[]{:S(2)}) collective-permute-start(f32[2,16,1,256]{3,2,1,0:T(1,128)S(1)} %get-tuple-element.15), channel_id=1, source_target_pairs={{16,0},{32,16},{48,32},{64,48},{80,64},{96,80},{112,96},{128,112},... | collective-permute-start | bytes 98312 | tf_op jit(solution)/shard_map/ppermute | solution.py:17
  56.8 11.5 %copy-start.3 = (bf16[2,2,16,16,256]{4,3,2,1,0:T(8,128)(2,1)S(1)}, bf16[2,2,16,16,256]{4,3,2,1,0:T(8,128)(2,1)}, u32[]{:S(2)}) copy-start(bf16[2,2,16,16,256]{4,3,2,1,0:T(8,128)(2,1)} %param.11) | copy-start | bytes 1572868
  56.8 4.8 %collective-permute-start.9 = (f32[2,16,1,256]{3,2,1,0:T(1,128)S(1)}, f32[2,16,1,256]{3,2,1,0:T(1,128)S(1)}, u32[]{:S(2)}, u32[]{:S(2)}) collective-permute-start(f32[2,16,1,256]{3,2,1,0:T(1,128)S(1)} %get-tuple-element.16), channel_id=1, source_target_pairs={{0,16},{16,32},{32,48},{48,64},{64,80},{80,96},{96,112},{112,128},... | collective-permute-start | bytes 98312 | tf_op jit(solution)/shard_map/ppermute | solution.py:15
  61.9 12.6 %collective-permute-start.10 = (f32[2,16,18,1]{3,2,1,0:T(8,128)S(1)}, f32[2,16,18,1]{3,2,1,0:T(8,128)S(1)}, u32[]{:S(2)}, u32[]{:S(2)}) collective-permute-start(f32[2,16,18,1]{3,2,1,0:T(8,128)S(1)} %get-tuple-element.11), channel_id=1, source_target_pairs={{1,0},{2,1},{3,2},{4,3},{5,4},{6,5},{7,6},{8,7},{9,8},{10,9},{11,1... | collective-permute-start | bytes 6920 | tf_op jit(solution)/shard_map/ppermute | solution.py:17
  63.2 13.0 %collective-permute-start.11 = (f32[2,16,18,1]{3,2,1,0:T(8,128)S(1)}, f32[2,16,18,1]{3,2,1,0:T(8,128)S(1)}, u32[]{:S(2)}, u32[]{:S(2)}) collective-permute-start(f32[2,16,18,1]{3,2,1,0:T(8,128)S(1)} %get-tuple-element.12), channel_id=1, source_target_pairs={{0,1},{1,2},{2,3},{3,4},{4,5},{5,6},{6,7},{7,8},{8,9},{9,10},{10,1... | collective-permute-start | bytes 6920 | tf_op jit(solution)/shard_map/ppermute | solution.py:15
  78.5 116.6 %all-gather.3.cloned.1.call-start = ((), (), s32[]{:S(2)}) async-start(), calls=%async_computation.3 | async-start | bytes 2228224 | tf_op jit(solution)/shard_map/all_gather | solution.py:105
  139.9 130.8 %all-reduce.5.cloned.1.call-start = ((), (), s32[]{:S(2)}) async-start(), calls=%async_computation.2 | async-start | bytes 524288 | tf_op jit(solution)/shard_map/psum | solution.py:116
  140.0 1.0 copy-start.4
  195.1 2.1 copy-start.9
  197.7 1.0 copy-start.5
  197.7 1.0 copy-start.6
  197.8 1.0 copy-start.8
Sparse Core Ops, SparseCore 0:
  78.6 59.6 reduce-scatter.1
  141.7 53.3 all-gather.2
  199.7 70.9 all-reduce.4
where the time goes:
time: 280 us; the launch traced here: 279 us
  waiting for transfers between devices  206 us (74%)
  starting transfers between devices  35.4 us (13%)
  between operations  14.1 us (5%)
  other arithmetic  12.9 us (5%)
  local copies, waits for them, and re-layouts  9.19 us (3%)
    psum x1, waiting for transfers between devices, shards(): sensitivity = lax.psum(partial_sens, 'sec')  70 us
    reduce_scatter x1, waiting for transfers between devices, shards(): lax.psum_scatter(jnp.stack([flow_x, flow_y]), 'sec', scatter_dimension=0,...  59.7 us
    all_gather x1, waiting for transfers between devices, shards(): piece = lax.all_gather(rounded, 'gy', axis=2, tiled=True)  52.4 us
    ppermute x6, starting transfers between devices, extended(): lax.ppermute(tail, axis, [(i, (i + 1) % count) for i in range(ends)])  21 us
    ppermute x6, starting transfers between devices, extended(): lax.ppermute(head, axis, [((i + 1) % count, i) for i in range(ends)])  14.3 us
    ppermute x6, waiting for transfers between devices, extended(): lax.ppermute(head, axis, [((i + 1) % count, i) for i in range(ends)])  13.5 us
    ppermute x6, waiting for transfers between devices, extended(): lax.ppermute(tail, axis, [(i, (i + 1) % count) for i in range(ends)])  10.6 us
  transfers between devices with their start and end apart: 15, of which 10 were waited for; matrix products, arithmetic and copies ran while one was open for 3% of the time, Pallas kernels for 0%

commit v1 on v0

--- a/solution.py
+++ b/solution.py
@@ -113,7 +113,7 @@
         "bkzxj,bkij->zxbi", picked, blocks, preferred_element_type=jnp.float32
     ).reshape(layers, rows_x, cols_y)
     partial_sens = heat_sens + head * head_gradient[0].astype(jnp.float32)
-    sensitivity = lax.psum(partial_sens, "sec")
+    sensitivity = jnp.sum(lax.all_gather(partial_sens, "sec"), axis=0)
     return (head[None], sensitivity)
 
 

time: 280 us -> 239 us (0.85)
  the two profiles are of different devices: /device:TPU:1 before, /device:TPU:32 now
where the time goes in v1:
time: 239 us; the launch traced here: 238 us
  waiting for transfers between devices  141 us (59%)
  blocking collectives  31.6 us (13%)
  starting transfers between devices  30.7 us (13%)
  between operations  14.5 us (6%)
  other arithmetic  13 us (5%)
  local copies, waits for them, and re-layouts  6.38 us (3%)
    all_gather x1, waiting for transfers between devices, shards(): piece = lax.all_gather(rounded, 'gy', axis=2, tiled=True)  61.1 us
    reduce_scatter x1, waiting for transfers between devices, shards(): lax.psum_scatter(jnp.stack([flow_x, flow_y]), 'sec', scatter_dimension=0,...  51.5 us
    all_gather x1, blocking collectives, shards(): sensitivity = jnp.sum(lax.all_gather(partial_sens, 'sec'), axis=0)  31.6 us
    ppermute x6, starting transfers between devices, extended(): lax.ppermute(tail, axis, [(i, (i + 1) % count) for i in range(ends)])  16.1 us
    ppermute x6, waiting for transfers between devices, extended(): lax.ppermute(head, axis, [((i + 1) % count, i) for i in range(ends)])  14.7 us
    ppermute x6, starting transfers between devices, extended(): lax.ppermute(head, axis, [((i + 1) % count, i) for i in range(ends)])  14.6 us
    ppermute x6, waiting for transfers between devices, extended(): lax.ppermute(tail, axis, [(i, (i + 1) % count) for i in range(ends)])  13.9 us
  transfers between devices with their start and end apart: 14, of which 9 were waited for; matrix products, arithmetic and copies ran while one was open for 3% of the time, Pallas kernels for 0%

profile of v1, /device:TPU:32, one launch (start us, length us, event | category | flops | bytes accessed | tf_op | source)
XLA Modules:
  0.0 238.3 jit_solution(9158095644743651502)
XLA Ops:
  7.2 0.0 copy-start
  7.2 0.0 reduce-scatter.2.cloned.1.call-start
  7.3 1.1 fusion.55
  8.3 1.9 collective-permute-start.2
  10.2 3.6 %collective-permute-start.3 = (f32[16,1,256]{2,1,0:T(1,128)S(1)}, f32[16,1,256]{2,1,0:T(1,128)S(1)}, u32[]{:S(2)}, u32[]{:S(2)}) collective-permute-start(f32[16,1,256]{2,1,0:T(1,128)S(1)} %get-tuple-element.30), channel_id=1, source_target_pairs={{16,0},{32,16},{48,32},{64,48},{80,64},{96,80},{112,96},{128,112},... | collective-permute-start | bytes 49160 | tf_op jit(solution)/shard_map/ppermute | solution.py:17
  13.9 1.1 fusion.53
  15.0 5.1 %collective-permute-start = (f32[2,16,1,256]{3,2,1,0:T(1,128)S(1)}, f32[2,16,1,256]{3,2,1,0:T(1,128)S(1)}, u32[]{:S(2)}, u32[]{:S(2)}) collective-permute-start(f32[2,16,1,256]{3,2,1,0:T(1,128)S(1)} %get-tuple-element.19), channel_id=1, source_target_pairs={{16,0},{32,16},{48,32},{64,48},{80,64},{96,80},{112,96},{128,112},... | collective-permute-start | bytes 98312 | tf_op jit(solution)/shard_map/ppermute | solution.py:17
  20.1 1.9 collective-permute-start.1
  22.1 0.7 slice_bitcast_fusion.3
  22.8 0.1 iota_compare_fusion.4
  22.9 1.1 multiply_bitcast_fusion.1
  24.0 0.1 broadcast_compare_fusion.1
  24.0 0.1 broadcast_and_fusion
  24.2 0.1 broadcast_compare_fusion
  24.3 0.1 pad_maximum_fusion.19
  24.4 0.1 fusion.54
  24.5 1.4 collective-permute-start.4
  25.9 1.3 collective-permute-start.5
  27.2 0.8 select_reduce_fusion
  28.0 3.1 %collective-permute-done.4 = f32[16,18,1]{2,1,0:T(8,128)S(1)} collective-permute-done((f32[16,18,1]{2,1,0:T(8,128)S(1)}, f32[16,18,1]{2,1,0:T(8,128)S(1)}, u32[]{:S(2)}, u32[]{:S(2)}) %collective-permute-start.4) | collective-permute-done | bytes 1184 | tf_op jit(solution)/shard_map/ppermute | solution.py:15
  31.2 4.2 %collective-permute-done.5 = f32[16,18,1]{2,1,0:T(8,128)S(1)} collective-permute-done((f32[16,18,1]{2,1,0:T(8,128)S(1)}, f32[16,18,1]{2,1,0:T(8,128)S(1)}, u32[]{:S(2)}, u32[]{:S(2)}) %collective-permute-start.5) | collective-permute-done | bytes 1184 | tf_op jit(solution)/shard_map/ppermute | solution.py:17
  35.3 0.4 select_maximum_fusion.8
  35.7 0.1 pad_maximum_fusion
  35.9 0.2 fusion.51
  36.0 2.9 %collective-permute-start.6 = (f32[2,16,18,1]{3,2,1,0:T(8,128)S(1)}, f32[2,16,18,1]{3,2,1,0:T(8,128)S(1)}, u32[]{:S(2)}, u32[]{:S(2)}) collective-permute-start(f32[2,16,18,1]{3,2,1,0:T(8,128)S(1)} %get-tuple-element.14), channel_id=1, source_target_pairs={{0,1},{1,2},{2,3},{3,4},{4,5},{5,6},{6,7},{7,8},{8,9},{9,10},{10,1... | collective-permute-start | bytes 6920 | tf_op jit(solution)/shard_map/ppermute | solution.py:15
  39.0 1.3 collective-permute-start.7
  40.3 0.6 fusion.40
  40.8 6.7 %collective-permute-done.6 = f32[2,16,18,1]{3,2,1,0:T(8,128)S(1)} collective-permute-done((f32[2,16,18,1]{3,2,1,0:T(8,128)S(1)}, f32[2,16,18,1]{3,2,1,0:T(8,128)S(1)}, u32[]{:S(2)}, u32[]{:S(2)}) %collective-permute-start.6) | collective-permute-done | bytes 2336 | tf_op jit(solution)/shard_map/ppermute | solution.py:15
  47.6 4.1 %collective-permute-done.7 = f32[2,16,18,1]{3,2,1,0:T(8,128)S(1)} collective-permute-done((f32[2,16,18,1]{3,2,1,0:T(8,128)S(1)}, f32[2,16,18,1]{3,2,1,0:T(8,128)S(1)}, u32[]{:S(2)}, u32[]{:S(2)}) %collective-permute-start.7) | collective-permute-done | bytes 2336 | tf_op jit(solution)/shard_map/ppermute | solution.py:17
  51.7 0.7 select_maximum_fusion.4
  52.5 1.1 add_multiply_fusion
  53.6 1.9 collective-permute-start.8
  55.5 2.5 %collective-permute-start.9 = (f32[2,16,1,256]{3,2,1,0:T(1,128)S(1)}, f32[2,16,1,256]{3,2,1,0:T(1,128)S(1)}, u32[]{:S(2)}, u32[]{:S(2)}) collective-permute-start(f32[2,16,1,256]{3,2,1,0:T(1,128)S(1)} %get-tuple-element.16), channel_id=1, source_target_pairs={{0,16},{16,32},{32,48},{48,64},{64,80},{80,96},{96,112},{112,128},... | collective-permute-start | bytes 98312 | tf_op jit(solution)/shard_map/ppermute | solution.py:15
  58.1 2.8 %collective-permute-done.9 = f32[2,16,1,256]{3,2,1,0:T(1,128)S(1)} collective-permute-done((f32[2,16,1,256]{3,2,1,0:T(1,128)S(1)}, f32[2,16,1,256]{3,2,1,0:T(1,128)S(1)}, u32[]{:S(2)}, u32[]{:S(2)}) %collective-permute-start.9) | collective-permute-done | bytes 32800 | tf_op jit(solution)/shard_map/ppermute | solution.py:15
  60.9 0.1 pad_maximum_fusion.1
  61.0 0.2 fusion.50
  61.2 1.3 collective-permute-start.10
  62.5 5.3 %collective-permute-start.11 = (f32[2,16,18,1]{3,2,1,0:T(8,128)S(1)}, f32[2,16,18,1]{3,2,1,0:T(8,128)S(1)}, u32[]{:S(2)}, u32[]{:S(2)}) collective-permute-start(f32[2,16,18,1]{3,2,1,0:T(8,128)S(1)} %get-tuple-element.12), channel_id=1, source_target_pairs={{0,1},{1,2},{2,3},{3,4},{4,5},{5,6},{6,7},{7,8},{8,9},{9,10},{10,1... | collective-permute-start | bytes 6920 | tf_op jit(solution)/shard_map/ppermute | solution.py:15
  67.8 0.6 fusion.3
  68.5 6.4 %collective-permute-done.10 = f32[2,16,18,1]{3,2,1,0:T(8,128)S(1)} collective-permute-done((f32[2,16,18,1]{3,2,1,0:T(8,128)S(1)}, f32[2,16,18,1]{3,2,1,0:T(8,128)S(1)}, u32[]{:S(2)}, u32[]{:S(2)}) %collective-permute-start.10) | collective-permute-done | bytes 2336 | tf_op jit(solution)/shard_map/ppermute | solution.py:17
  74.9 1.2 collective-permute-done.11
  76.0 1.3 fusion.6
  77.4 0.1 add_bitcast_fusion
  77.4 0.8 pad_maximum_fusion.18
  78.3 0.0 reduce-scatter.2.cloned.1.call-update
  78.3 0.0 all-gather.3.cloned.1.call-start
  78.3 51.5 %reduce-scatter.2.cloned.1.call-done = f32[1,16,16,256]{3,2,1,0:T(8,128)} async-done(((f32[2,16,16,256]{3,2,1,0:T(8,128)}), f32[1,16,16,256]{3,2,1,0:T(8,128)}) %reduce-scatter.2.cloned.1.call-update) | async-done | bytes 262160 | tf_op jit(solution)/shard_map/reduce_scatter | solution.py:102
  129.9 1.6 convert_element_type.39
  131.5 0.0 all-gather.3.cloned.1.call-update
  131.5 0.7 select_maximum_fusion
  132.3 0.3 copy-done.4
  132.6 1.7 fusion.8
  134.3 61.1 %all-gather.3.cloned.1.call-done = bf16[1,16,16,4096]{3,2,1,0:T(8,128)(2,1)} async-done(((bf16[1,16,16,256]{3,2,1,0:T(8,128)(2,1)}), bf16[1,16,16,4096]{3,2,1,0:T(8,128)(2,1)}) %all-gather.3.cloned.1.call-update) | async-done | bytes 2097168 | tf_op jit(solution)/shard_map/all_gather | solution.py:105
  195.4 2.1 copy.20
  197.5 0.5 convolution_convert_fusion
  198.0 0.4 convolution_bitcast_fusion
  198.4 0.2 copy.16
  198.6 0.2 broadcast_in_dim_reshape.3
  198.9 0.1 copy-done.5
  198.9 0.1 copy-done.6
  199.0 0.0 copy-done.9
  199.0 0.1 bitcast_add_fusion
  199.1 31.6 %all_gather.8 = f32[2,16,16,256]{3,2,1,0:T(8,128)S(1)} all-gather(f32[1,16,16,256]{3,2,1,0:T(8,128)S(1)} %bitcast_add_fusion), channel_id=1, replica_groups=mesh['sec'=2,'gx'=16,'gy'=16] {'sec'}, dimensions={0}, use_global_device_ids=true | all-gather | bytes 786432 | tf_op jit(solution)/shard_map/all_gather | solution.py:116
  230.7 0.7 reduce_sum.79
  (29 shorter events, 0.1 us)
Async XLA Ops:
  7.2 190.8 %copy-start = (bf16[2,7,128,128]{3,2,1,0:T(8,128)(2,1)S(1)}, bf16[2,7,128,128]{3,2,1,0:T(8,128)(2,1)}, u32[]{:S(2)}) copy-start(bf16[2,7,128,128]{3,2,1,0:T(8,128)(2,1)} %param.18) | copy-start | bytes 1376260
  7.2 17.1 %copy-start.2 = (f32[16,16,256]{2,1,0:T(8,128)S(1)}, f32[16,16,256]{2,1,0:T(8,128)}, u32[]{:S(2)}) copy-start(f32[16,16,256]{2,1,0:T(8,128)} %param.12) | copy-start | bytes 786436
  7.2 16.7 %copy-start.8 = (s32[16,16,256]{2,1,0:T(8,128)S(1)}, s32[16,16,256]{2,1,0:T(8,128)}, u32[]{:S(2)}) copy-start(s32[16,16,256]{2,1,0:T(8,128)} %param.14) | copy-start | bytes 786436
  7.2 17.0 %copy-start.11 = (f32[2,2,8]{2,1,0:T(2,128)S(1)}, f32[2,2,8]{2,1,0:T(2,128)}, u32[]{:S(2)}) copy-start(f32[2,2,8]{2,1,0:T(2,128)} %param.16) | copy-start | bytes 388
  7.2 122.7 %reduce-scatter.2.cloned.1.call-start = ((), (), s32[]{:S(2)}) async-start(), calls=%async_computation.1 | async-start | bytes 786432 | tf_op jit(solution)/shard_map/reduce_scatter | solution.py:102
  8.3 15.9 %collective-permute-start.2 = (f32[16,1,256]{2,1,0:T(1,128)S(1)}, f32[16,1,256]{2,1,0:T(1,128)S(1)}, u32[]{:S(2)}, u32[]{:S(2)}) collective-permute-start(f32[16,1,256]{2,1,0:T(1,128)S(1)} %get-tuple-element.29), channel_id=1, source_target_pairs={{0,16},{16,32},{32,48},{48,64},{64,80},{80,96},{96,112},{112,128},... | collective-permute-start | bytes 49160 | tf_op jit(solution)/shard_map/ppermute | solution.py:15
  10.2 14.0 %collective-permute-start.3 = (f32[16,1,256]{2,1,0:T(1,128)S(1)}, f32[16,1,256]{2,1,0:T(1,128)S(1)}, u32[]{:S(2)}, u32[]{:S(2)}) collective-permute-start(f32[16,1,256]{2,1,0:T(1,128)S(1)} %get-tuple-element.30), channel_id=1, source_target_pairs={{16,0},{32,16},{48,32},{64,48},{80,64},{96,80},{112,96},{128,112},... | collective-permute-start | bytes 49160 | tf_op jit(solution)/shard_map/ppermute | solution.py:17
  15.0 20.7 %collective-permute-start = (f32[2,16,1,256]{3,2,1,0:T(1,128)S(1)}, f32[2,16,1,256]{3,2,1,0:T(1,128)S(1)}, u32[]{:S(2)}, u32[]{:S(2)}) collective-permute-start(f32[2,16,1,256]{3,2,1,0:T(1,128)S(1)} %get-tuple-element.19), channel_id=1, source_target_pairs={{16,0},{32,16},{48,32},{64,48},{80,64},{96,80},{112,96},{128,112},... | collective-permute-start | bytes 98312 | tf_op jit(solution)/shard_map/ppermute | solution.py:17
  20.1 15.6 %collective-permute-start.1 = (f32[2,16,1,256]{3,2,1,0:T(1,128)S(1)}, f32[2,16,1,256]{3,2,1,0:T(1,128)S(1)}, u32[]{:S(2)}, u32[]{:S(2)}) collective-permute-start(f32[2,16,1,256]{3,2,1,0:T(1,128)S(1)} %get-tuple-element.20), channel_id=1, source_target_pairs={{0,16},{16,32},{32,48},{48,64},{64,80},{80,96},{96,112},{112,128},... | collective-permute-start | bytes 98312 | tf_op jit(solution)/shard_map/ppermute | solution.py:15
  24.3 11.4 %copy-start.1 = (f32[2,16,16,256]{3,2,1,0:T(8,128)S(1)}, f32[2,16,16,256]{3,2,1,0:T(8,128)}, u32[]{:S(2)}) copy-start(f32[2,16,16,256]{3,2,1,0:T(8,128)} %param.10) | copy-start | bytes 1572868
  24.5 6.7 %collective-permute-start.4 = (f32[16,18,1]{2,1,0:T(8,128)S(1)}, f32[16,18,1]{2,1,0:T(8,128)S(1)}, u32[]{:S(2)}, u32[]{:S(2)}) collective-permute-start(f32[16,18,1]{2,1,0:T(8,128)S(1)} %get-tuple-element.22), channel_id=1, source_target_pairs={{0,1},{1,2},{2,3},{3,4},{4,5},{5,6},{6,7},{7,8},{8,9},{9,10},{10,1... | collective-permute-start | bytes 3464 | tf_op jit(solution)/shard_map/ppermute | solution.py:15
  25.9 9.4 %collective-permute-start.5 = (f32[16,18,1]{2,1,0:T(8,128)S(1)}, f32[16,18,1]{2,1,0:T(8,128)S(1)}, u32[]{:S(2)}, u32[]{:S(2)}) collective-permute-start(f32[16,18,1]{2,1,0:T(8,128)S(1)} %get-tuple-element.21), channel_id=1, source_target_pairs={{1,0},{2,1},{3,2},{4,3},{5,4},{6,5},{7,6},{8,7},{9,8},{10,9},{11,1... | collective-permute-start | bytes 3464 | tf_op jit(solution)/shard_map/ppermute | solution.py:17
  36.0 11.5 %collective-permute-start.6 = (f32[2,16,18,1]{3,2,1,0:T(8,128)S(1)}, f32[2,16,18,1]{3,2,1,0:T(8,128)S(1)}, u32[]{:S(2)}, u32[]{:S(2)}) collective-permute-start(f32[2,16,18,1]{3,2,1,0:T(8,128)S(1)} %get-tuple-element.14), channel_id=1, source_target_pairs={{0,1},{1,2},{2,3},{3,4},{4,5},{5,6},{6,7},{7,8},{8,9},{9,10},{10,1... | collective-permute-start | bytes 6920 | tf_op jit(solution)/shard_map/ppermute | solution.py:15
  39.0 12.7 %collective-permute-start.7 = (f32[2,16,18,1]{3,2,1,0:T(8,128)S(1)}, f32[2,16,18,1]{3,2,1,0:T(8,128)S(1)}, u32[]{:S(2)}, u32[]{:S(2)}) collective-permute-start(f32[2,16,18,1]{3,2,1,0:T(8,128)S(1)} %get-tuple-element.13), channel_id=1, source_target_pairs={{1,0},{2,1},{3,2},{4,3},{5,4},{6,5},{7,6},{8,7},{9,8},{10,9},{11,1... | collective-permute-start | bytes 6920 | tf_op jit(solution)/shard_map/ppermute | solution.py:17
  53.6 4.5 %collective-permute-start.8 = (f32[2,16,1,256]{3,2,1,0:T(1,128)S(1)}, f32[2,16,1,256]{3,2,1,0:T(1,128)S(1)}, u32[]{:S(2)}, u32[]{:S(2)}) collective-permute-start(f32[2,16,1,256]{3,2,1,0:T(1,128)S(1)} %get-tuple-element.15), channel_id=1, source_target_pairs={{16,0},{32,16},{48,32},{64,48},{80,64},{96,80},{112,96},{128,112},... | collective-permute-start | bytes 98312 | tf_op jit(solution)/shard_map/ppermute | solution.py:17
  55.5 12.3 %copy-start.3 = (bf16[2,2,16,16,256]{4,3,2,1,0:T(8,128)(2,1)S(1)}, bf16[2,2,16,16,256]{4,3,2,1,0:T(8,128)(2,1)}, u32[]{:S(2)}) copy-start(bf16[2,2,16,16,256]{4,3,2,1,0:T(8,128)(2,1)} %param.11) | copy-start | bytes 1572868
  55.5 5.4 %collective-permute-start.9 = (f32[2,16,1,256]{3,2,1,0:T(1,128)S(1)}, f32[2,16,1,256]{3,2,1,0:T(1,128)S(1)}, u32[]{:S(2)}, u32[]{:S(2)}) collective-permute-start(f32[2,16,1,256]{3,2,1,0:T(1,128)S(1)} %get-tuple-element.16), channel_id=1, source_target_pairs={{0,16},{16,32},{32,48},{48,64},{64,80},{80,96},{96,112},{112,128},... | collective-permute-start | bytes 98312 | tf_op jit(solution)/shard_map/ppermute | solution.py:15
  61.2 13.7 %collective-permute-start.10 = (f32[2,16,18,1]{3,2,1,0:T(8,128)S(1)}, f32[2,16,18,1]{3,2,1,0:T(8,128)S(1)}, u32[]{:S(2)}, u32[]{:S(2)}) collective-permute-start(f32[2,16,18,1]{3,2,1,0:T(8,128)S(1)} %get-tuple-element.11), channel_id=1, source_target_pairs={{1,0},{2,1},{3,2},{4,3},{5,4},{6,5},{7,6},{8,7},{9,8},{10,9},{11,1... | collective-permute-start | bytes 6920 | tf_op jit(solution)/shard_map/ppermute | solution.py:17
  62.5 13.6 %collective-permute-start.11 = (f32[2,16,18,1]{3,2,1,0:T(8,128)S(1)}, f32[2,16,18,1]{3,2,1,0:T(8,128)S(1)}, u32[]{:S(2)}, u32[]{:S(2)}) collective-permute-start(f32[2,16,18,1]{3,2,1,0:T(8,128)S(1)} %get-tuple-element.12), channel_id=1, source_target_pairs={{0,1},{1,2},{2,3},{3,4},{4,5},{5,6},{6,7},{7,8},{8,9},{9,10},{10,1... | collective-permute-start | bytes 6920 | tf_op jit(solution)/shard_map/ppermute | solution.py:15
  78.3 117.1 %all-gather.3.cloned.1.call-start = ((), (), s32[]{:S(2)}) async-start(), calls=%async_computation.2 | async-start | bytes 2228224 | tf_op jit(solution)/shard_map/all_gather | solution.py:105
  131.5 1.0 copy-start.4
  195.4 2.1 copy-start.10
  198.0 1.0 copy-start.5
  198.0 1.0 copy-start.6
  198.0 1.0 copy-start.9
  198.9 32.6 %copy-start.7 = (f32[1,16,16,256]{3,2,1,0:T(8,128)}, f32[1,16,16,256]{3,2,1,0:T(8,128)S(1)}, u32[]{:S(2)}) copy-start(f32[1,16,16,256]{3,2,1,0:T(8,128)S(1)} %broadcast_in_dim_reshape.3) | copy-start | bytes 786436
Sparse Core Ops, SparseCore 0:
  78.4 51.4 reduce-scatter.1
  133.9 61.4 all-gather.2
